TPU v7x, 512 devices: a whole 4x8x8 slice. The times are simulated.
512 devices in a mesh: gx: 8 (over z), gy: 16 (over y_hi, x, core), gz: 4 (over y_lo).
Axes of the slice: x: 4, y: 8 (y_hi: 2, y_lo: 4; y = y_hi * 4 + y_lo), z: 8, core: 2. Of those that a mesh axis runs over, the one named last changes fastest.
Arguments:
- field: bfloat16 [64, 32, 256, 1024], P(None, 'gz', 'gy', 'gx'), may hold values from -8 to 8
- conv_first: bfloat16 [3, 3, 3, 64, 128], replicated, may hold values from -0.15625 to 0.15625
- norm_gain: float32 [128], replicated, may hold values from 0.5 to 1.5
- norm_shift: float32 [128], replicated, may hold values from -3 to 3
- conv_second: bfloat16 [3, 3, 3, 128, 128], replicated, may hold values from -0.109375 to 0.109375
Outputs:
- result: bfloat16 [128, 16, 128, 512], P(None, 'gz', 'gy', 'gx')
All inputs are finite; a program needn't handle non-finite values.
Results may differ from a plain program's by a relative error of at most 0.0017.
The roundings to bfloat16 on the way count: a program that leaves them out, or rounds other values in their place, can miss the bound.
Values may be sent and summed in bfloat16 or wider, within the bound.
A program may use at most 128 MiB of HBM per device.

v0:
```python
import jax
import jax.numpy as jnp
from jax import lax
from jax.sharding import PartitionSpec as P

NEWTON = 5
epsilon = 1e-05
leak_slope = 0.2
dimension_spec = ("NCDHW", "DHWIO", "NCDHW")


def from_behind(value, axis, steps):
    count = lax.axis_size(axis)
    leading, last = (max(0, -steps), min(count, count - steps))
    return lax.ppermute(value, axis, [(source, source + steps) for source in range(leading, last)])


def extended_2(value, sides, width):
    for axis, dim in sides:
        size, length = (lax.axis_size(axis), value.shape[dim])
        up = [(i, (i + 1) % size) for i in range(size - 1)]
        down = [(j, i) for i, j in up]
        last = lax.slice_in_dim(value, length - width, length, axis=dim)
        leading = lax.slice_in_dim(value, 0, width, axis=dim)
        before = lax.ppermute(last, axis, up)
        after = lax.ppermute(leading, axis, down)
        value = jnp.concatenate([before, value, after], axis=dim)
    return value


def convolve(volume, kernel, strides):
    return lax.conv_general_dilated(
        volume[None],
        kernel,
        strides,
        ((0, 0), (0, 0), (0, 0)),
        dimension_numbers=dimension_spec,
        preferred_element_type=jnp.float32,
    )[0]


def newton_whitener(covariance):
    trace_value = jnp.trace(covariance, axis1=1, axis2=2)
    scaled = covariance / trace_value[:, None, None]
    identity = jnp.broadcast_to(jnp.eye(covariance.shape[-1], dtype=jnp.float32), covariance.shape)
    newton_mat = identity
    for repeat in range(NEWTON):
        square = jnp.einsum("gij,gjk->gik", newton_mat, newton_mat, precision=lax.Precision.HIGHEST)
        cubed = jnp.einsum("gij,gjk->gik", square, newton_mat, precision=lax.Precision.HIGHEST)
        newton_mat = 1.5 * newton_mat - 0.5 * jnp.einsum(
            "gij,gjk->gik", cubed, scaled, precision=lax.Precision.HIGHEST
        )
    return newton_mat / jnp.sqrt(trace_value)[:, None, None]


def whiten(block, average, whitener, norm_gain, norm_shift):
    shape = block.shape
    grouped = block.reshape(2, shape[0] // 2, -1) - average[:, :, None]
    mixed = jnp.einsum("gij,gjm->gim", whitener, grouped, precision=lax.Precision.HIGHEST).reshape(
        shape
    )
    scaled = mixed * norm_gain[:, None, None, None] + norm_shift[:, None, None, None]
    return jnp.where(scaled >= 0, scaled, leak_slope * scaled).astype(jnp.bfloat16)


def body(field, conv_first, norm_gain, norm_shift, conv_second):
    border = field[:, :, :, -1:]
    arrived = from_behind(border, "gx", 1)
    extended = jnp.concatenate([arrived, field], axis=3)
    border = extended[:, :, -1:, :]
    arrived = from_behind(border, "gy", 1)
    extended = jnp.concatenate([arrived, extended], axis=2)
    border = extended[:, -1:, :, :]
    arrived = from_behind(border, "gz", 1)
    extended = jnp.concatenate([arrived, extended], axis=1)
    features = convolve(extended, conv_first, (2, 2, 2))
    channels, depth, height, width = features.shape
    grouped = features.reshape(2, channels // 2, -1)
    total_cells = grouped.shape[2] * lax.axis_size("gx") * lax.axis_size("gy") * lax.axis_size("gz")
    identity = jnp.eye(channels // 2, dtype=jnp.float32)[None]
    channel_total = lax.psum(jnp.sum(grouped, axis=2), ("gx", "gy", "gz"))
    average = channel_total / total_cells
    centered = grouped - average[:, :, None]
    moments = jnp.einsum("gim,gjm->gij", centered, centered, precision=lax.Precision.HIGHEST)
    covariance = lax.psum(moments, ("gx", "gy", "gz")) / total_cells
    covariance = covariance + epsilon * identity
    whitener = newton_whitener(covariance)
    activation = whiten(features, average, whitener, norm_gain, norm_shift)
    padded = extended_2(activation, (("gx", 3), ("gy", 2), ("gz", 1)), 1)
    return convolve(padded, conv_second, (1, 1, 1)).astype(jnp.bfloat16)


def solution(mesh):
    in_specs = (P(None, "gz", "gy", "gx"), P(), P(), P(), P())
    out_specs = P(None, "gz", "gy", "gx")
    return jax.shard_map(body, mesh=mesh, in_specs=in_specs, out_specs=out_specs, check_vma=False)
```

profile of v0, /device:TPU:15, one launch (start us, length us, event | category | flops | bytes accessed | tf_op | source)
XLA Modules:
  0.0 372.0 jit_solution(6454287989513441158)
XLA Ops:
  4.7 4.0 %collective-permute-start = (bf16[64,8,16,1]{0,2,3,1:T(8,128)(2,1)S(1)}, bf16[64,8,16,1]{0,2,3,1:T(8,128)(2,1)S(1)}, u32[]{:S(2)}, u32[]{:S(2)}) collective-permute-start(bf16[64,8,16,1]{0,2,3,1:T(8,128)(2,1)S(1)} %copy.63), channel_id=1, source_target_pairs={{0,64},{64,128},{128,192},{192,256},{256,320},{320,384},{384,448},... | collective-permute-start | bytes 49160 | tf_op jit(solution)/shard_map/ppermute | solution.py:15
  11.0 4.3 %copy.42 = bf16[64,8,16,1]{3,1,2,0:T(8,128)(2,1)} copy(bf16[64,8,16,1]{0,2,3,1:T(8,128)(2,1)S(1)} %collective-permute-done) | data formatting | bytes 32768 | tf_op jit(solution)/shard_map/ppermute | solution.py:15
  16.6 7.3 %collective-permute-start.1 = (bf16[64,8,1,129]{3,1,2,0:T(8,128)(2,1)S(1)}, bf16[64,8,1,129]{3,1,2,0:T(8,128)(2,1)S(1)}, u32[]{:S(2)}, u32[]{:S(2)}) collective-permute-start(bf16[64,8,1,129]{3,1,2,0:T(8,128)(2,1)S(1)} %pad_maximum_fusion.6), channel_id=1, source_target_pairs={{0,4},{4,8},{8,12},{12,16},{16,20},{20,24},{24,28},{28,32},{32,36}... | collective-permute-start | bytes 396296 | tf_op jit(solution)/shard_map/ppermute | solution.py:15
  23.9 6.1 %collective-permute-done.1 = bf16[64,8,1,129]{3,1,2,0:T(8,128)(2,1)S(1)} collective-permute-done((bf16[64,8,1,129]{3,1,2,0:T(8,128)(2,1)S(1)}, bf16[64,8,1,129]{3,1,2,0:T(8,128)(2,1)S(1)}, u32[]{:S(2)}, u32[]{:S(2)}) %collective-permute-start.1) | collective-permute-done | bytes 132128 | tf_op jit(solution)/shard_map/ppermute | solution.py:15
  32.6 2.6 collective-permute-start.2
  35.5 9.1 %collective-permute-done.2 = bf16[64,1,17,129]{3,0,2,1:T(8,128)(2,1)S(1)} collective-permute-done((bf16[64,1,17,129]{3,0,2,1:T(8,128)(2,1)S(1)}, bf16[64,1,17,129]{3,0,2,1:T(8,128)(2,1)S(1)}, u32[]{:S(2)}, u32[]{:S(2)}) %collective-permute-start.2) | collective-permute-done | bytes 280736 | tf_op jit(solution)/shard_map/ppermute | solution.py:15
  45.4 7.5 %maximum_bitcast_fusion = bf16[64,9,17,1,129]{4,1,2,0,3:T(8,128)(2,1)} fusion(bf16[64,8,16,128]{3,1,2,0:T(8,128)(2,1)S(1)} %copy.43, bf16[64,8,16,1]{3,1,2,0:T(8,128)(2,1)S(1)} %copy-done.1, bf16[64,8,1,129]{3,1,2,0:T(8,128)(2,1)S(1)} %collective-permute-done.1, bf16[64,1,17,129]{3,1,2,0:T(2,128)(2,1)S(1)} %copy.45), kind=kLoop, calls=%fused_computation.2 | loop fusion | flops 10105344 | bytes 5052672 | tf_op jit(solution)/shard_map/broadcast_in_dim | solution.py:33
  52.9 14.9 %copy.64 = bf16[64,9,17,1,129]{0,4,2,1,3:T(8,128)(2,1)} copy(bf16[64,9,17,1,129]{4,1,2,0,3:T(8,128)(2,1)} %maximum_bitcast_fusion) | data formatting | bytes 5052672
  67.8 6.0 %pad.clone = bf16[64,9,17,1,144]{0,4,2,1,3:T(8,128)(2,1)} pad(bf16[64,9,17,1,129]{0,4,2,1,3:T(8,128)(2,1)} %copy.64, bf16[]{:T(256)} %constant.22), padding=0_0x0_0x0_0x0_0x0_15 | pad | bytes 5346434 | tf_op jit(solution)/shard_map/broadcast_in_dim | solution.py:33
  73.9 10.6 %reshape.24 = bf16[64,9,17,1,8,18]{0,5,4,2,1,3:T(8,128)(2,1)} reshape(bf16[64,9,17,1,144]{0,4,2,1,3:T(8,128)(2,1)} %pad.clone) | data formatting | bytes 5640192 | tf_op jit(solution)/shard_map/conv_general_dilated | solution.py:32
  84.5 4.3 %copy.48 = bf16[64,9,17,1,8,18]{0,4,5,2,1,3:T(8,128)(2,1)S(1)} copy(bf16[64,9,17,1,8,18]{0,5,4,2,1,3:T(8,128)(2,1)} %reshape.24) | data formatting | bytes 5640192 | tf_op jit(solution)/shard_map/conv_general_dilated | solution.py:32
  89.0 2.9 select_reduce_fusion
  92.2 3.0 copy.50
  97.3 102.7 %psum.14 = f32[2,64]{1,0:T(2,128)S(1)} all-reduce(f32[2,64]{1,0:T(2,128)S(1)} %reduce_sum.22), channel_id=1, replica_groups=mesh['gx'=8,'gy'=16,'gz'=4] {'gx','gy','gz'}, use_global_device_ids=true, to_apply=%region_1.0 | all-reduce | flops 128 | bytes 1024 | tf_op jit(solution)/shard_map/psum | solution.py:81
  201.3 94.6 %psum.15 = f32[2,64,64]{2,1,0:T(8,128)S(1)} all-reduce(f32[2,64,64]{2,1,0:T(8,128)S(1)} %fusion.32), channel_id=1, replica_groups=mesh['gx'=8,'gy'=16,'gz'=4] {'gx','gy','gz'}, use_global_device_ids=true, to_apply=%region_2.0 | all-reduce | flops 8192 | bytes 65536 | tf_op jit(solution)/shard_map/psum | solution.py:85
  317.4 3.7 pad_maximum_fusion.5
  321.0 8.1 %collective-permute-start.5 = (bf16[128,4,1,66]{3,2,1,0:T(2,128)(2,1)S(1)}, bf16[128,4,1,66]{3,2,1,0:T(2,128)(2,1)S(1)}, u32[]{:S(2)}, u32[]{:S(2)}) collective-permute-start(bf16[128,4,1,66]{3,2,1,0:T(2,128)(2,1)S(1)} %get-tuple-element.5), channel_id=1, source_target_pairs={{0,4},{4,8},{8,12},{12,16},{16,20},{20,24},{24,28},{28,32},{32,36}... | collective-permute-start | bytes 202760 | tf_op jit(solution)/shard_map/ppermute | solution.py:25
  331.0 4.2 %collective-permute-done.5 = bf16[128,4,1,66]{3,2,1,0:T(2,128)(2,1)S(1)} collective-permute-done((bf16[128,4,1,66]{3,2,1,0:T(2,128)(2,1)S(1)}, bf16[128,4,1,66]{3,2,1,0:T(2,128)(2,1)S(1)}, u32[]{:S(2)}, u32[]{:S(2)}) %collective-permute-start.5) | collective-permute-done | bytes 67616 | tf_op jit(solution)/shard_map/ppermute | solution.py:25
  335.2 10.4 %collective-permute-done.6 = bf16[128,4,1,66]{3,2,1,0:T(2,128)(2,1)S(1)} collective-permute-done((bf16[128,4,1,66]{3,2,1,0:T(2,128)(2,1)S(1)}, bf16[128,4,1,66]{3,2,1,0:T(2,128)(2,1)S(1)}, u32[]{:S(2)}, u32[]{:S(2)}) %collective-permute-start.6) | collective-permute-done | bytes 67616 | tf_op jit(solution)/shard_map/ppermute | solution.py:26
  345.6 3.3 pad_maximum_fusion
  351.4 3.5 collective-permute-start.7
  357.0 3.1 copy.56
  361.9 3.1 collective-permute-done.8
  366.4 4.3 %fusion.18 = bf16[4,8,8,9,128]{4,2,3,1,0:T(8,128)(2,1)S(1)} fusion(bf16[3,3,3,128,128]{4,3,2,1,0:T(8,128)(2,1)S(1)} %copy-done, bf16[128,6,10,1,7,2]{0,4,5,2,1,3:T(8,128)(2,1)S(1)} %slice.46, bf16[128,6,10,1,8,9]{0,4,5,2,1,3:T(8,128)(2,1)S(1)} %copy.60, pred[8,9]{0,1:T(8,128)(4,1)S(1)} %copy-done.7), kind=kOutput, calls=%fused_computation.19 | convolution fusion | flops 2043076608 | bytes 2795592 | tf_op jit(solution)/shard_map/conv_general_dilated | solution.py:32
  (79 shorter events, 47.9 us)
Async XLA Ops:
  0.0 366.4 %copy-start = (bf16[3,3,3,128,128]{4,3,2,1,0:T(8,128)(2,1)S(1)}, bf16[3,3,3,128,128]{4,3,2,1,0:T(8,128)(2,1)}, u32[]{:S(2)}) copy-start(bf16[3,3,3,128,128]{4,3,2,1,0:T(8,128)(2,1)} %param.9) | copy-start | bytes 2654212
  4.7 6.4 %collective-permute-start = (bf16[64,8,16,1]{0,2,3,1:T(8,128)(2,1)S(1)}, bf16[64,8,16,1]{0,2,3,1:T(8,128)(2,1)S(1)}, u32[]{:S(2)}, u32[]{:S(2)}) collective-permute-start(bf16[64,8,16,1]{0,2,3,1:T(8,128)(2,1)S(1)} %copy.63), channel_id=1, source_target_pairs={{0,64},{64,128},{128,192},{192,256},{256,320},{320,384},{384,448},... | collective-permute-start | bytes 49160 | tf_op jit(solution)/shard_map/ppermute | solution.py:15
  15.4 14.6 %copy-start.1 = (bf16[64,8,16,1]{3,1,2,0:T(8,128)(2,1)S(1)}, bf16[64,8,16,1]{3,1,2,0:T(8,128)(2,1)}, u32[]{:S(2)}) copy-start(bf16[64,8,16,1]{3,1,2,0:T(8,128)(2,1)} %copy.42) | copy-start | bytes 49156
  16.6 13.4 %collective-permute-start.1 = (bf16[64,8,1,129]{3,1,2,0:T(8,128)(2,1)S(1)}, bf16[64,8,1,129]{3,1,2,0:T(8,128)(2,1)S(1)}, u32[]{:S(2)}, u32[]{:S(2)}) collective-permute-start(bf16[64,8,1,129]{3,1,2,0:T(8,128)(2,1)S(1)} %pad_maximum_fusion.6), channel_id=1, source_target_pairs={{0,4},{4,8},{8,12},{12,16},{16,20},{20,24},{24,28},{28,32},{32,36}... | collective-permute-start | bytes 396296 | tf_op jit(solution)/shard_map/ppermute | solution.py:15
  32.6 11.9 %collective-permute-start.2 = (bf16[64,1,17,129]{3,0,2,1:T(8,128)(2,1)S(1)}, bf16[64,1,17,129]{3,0,2,1:T(8,128)(2,1)S(1)}, u32[]{:S(2)}, u32[]{:S(2)}) collective-permute-start(bf16[64,1,17,129]{3,0,2,1:T(8,128)(2,1)S(1)} %copy.44), channel_id=1, source_target_pairs={{0,1},{1,2},{2,3},{4,5},{5,6},{6,7},{8,9},{9,10},{10,11},{12,13},{... | collective-permute-start | bytes 842120 | tf_op jit(solution)/shard_map/ppermute | solution.py:15
  84.5 4.5 %copy-start.6 = (bf16[3,3,3,64,128]{4,3,2,1,0:T(8,128)(2,1)S(1)}, bf16[3,3,3,64,128]{4,3,2,1,0:T(8,128)(2,1)}, u32[]{:S(2)}) copy-start(bf16[3,3,3,64,128]{4,3,2,1,0:T(8,128)(2,1)} %param.6) | copy-start | bytes 1327108
  84.5 4.5 %copy-start.7 = (pred[8,9]{0,1:T(8,128)(4,1)S(1)}, pred[8,9]{0,1:T(8,128)(4,1)}, u32[]{:S(2)}) copy-start(pred[8,9]{0,1:T(8,128)(4,1)} %constant.31) | copy-start | bytes 220
  299.7 2.2 copy-start.4
  299.7 2.2 copy-start.5
  307.7 4.3 %collective-permute-start.3 = (bf16[128,4,8,1]{0,2,3,1:T(8,128)(2,1)S(1)}, bf16[128,4,8,1]{0,2,3,1:T(8,128)(2,1)S(1)}, u32[]{:S(2)}, u32[]{:S(2)}) collective-permute-start(bf16[128,4,8,1]{0,2,3,1:T(8,128)(2,1)S(1)} %copy.51), channel_id=1, source_target_pairs={{0,64},{64,128},{128,192},{192,256},{256,320},{320,384},{384,448},... | collective-permute-start | bytes 24584 | tf_op jit(solution)/shard_map/ppermute | solution.py:25
  310.6 4.4 %collective-permute-start.4 = (bf16[128,4,8,1]{0,2,3,1:T(8,128)(2,1)S(1)}, bf16[128,4,8,1]{0,2,3,1:T(8,128)(2,1)S(1)}, u32[]{:S(2)}, u32[]{:S(2)}) collective-permute-start(bf16[128,4,8,1]{0,2,3,1:T(8,128)(2,1)S(1)} %copy.52), channel_id=1, source_target_pairs={{64,0},{128,64},{192,128},{256,192},{320,256},{384,320},{448,384},... | collective-permute-start | bytes 24584 | tf_op jit(solution)/shard_map/ppermute | solution.py:26
  317.4 28.2 %copy-start.3 = (bf16[128,4,8,1]{3,2,1,0:T(8,128)(2,1)S(1)}, bf16[128,4,8,1]{3,2,1,0:T(8,128)(2,1)}, u32[]{:S(2)}) copy-start(bf16[128,4,8,1]{3,2,1,0:T(8,128)(2,1)} %copy.54) | copy-start | bytes 24580
  321.0 14.2 %collective-permute-start.5 = (bf16[128,4,1,66]{3,2,1,0:T(2,128)(2,1)S(1)}, bf16[128,4,1,66]{3,2,1,0:T(2,128)(2,1)S(1)}, u32[]{:S(2)}, u32[]{:S(2)}) collective-permute-start(bf16[128,4,1,66]{3,2,1,0:T(2,128)(2,1)S(1)} %get-tuple-element.5), channel_id=1, source_target_pairs={{0,4},{4,8},{8,12},{12,16},{16,20},{20,24},{24,28},{28,32},{32,36}... | collective-permute-start | bytes 202760 | tf_op jit(solution)/shard_map/ppermute | solution.py:25
  329.1 16.5 %collective-permute-start.6 = (bf16[128,4,1,66]{3,2,1,0:T(2,128)(2,1)S(1)}, bf16[128,4,1,66]{3,2,1,0:T(2,128)(2,1)S(1)}, u32[]{:S(2)}, u32[]{:S(2)}) collective-permute-start(bf16[128,4,1,66]{3,2,1,0:T(2,128)(2,1)S(1)} %get-tuple-element.6), channel_id=1, source_target_pairs={{4,0},{8,4},{12,8},{16,12},{20,16},{24,20},{28,24},{32,28},{36,32}... | collective-permute-start | bytes 202760 | tf_op jit(solution)/shard_map/ppermute | solution.py:26
  348.9 1.3 copy-start.2
  351.4 10.1 %collective-permute-start.7 = (bf16[128,1,10,66]{3,2,1,0:T(8,128)(2,1)}, bf16[128,1,10,66]{3,2,1,0:T(8,128)(2,1)S(1)}, u32[]{:S(2)}, u32[]{:S(2)}) collective-permute-start(bf16[128,1,10,66]{3,2,1,0:T(8,128)(2,1)} %get-tuple-element.7), channel_id=1, source_target_pairs={{0,1},{1,2},{2,3},{4,5},{5,6},{6,7},{8,9},{9,10},{10,11},{12,13},{... | collective-permute-start | bytes 506888 | tf_op jit(solution)/shard_map/ppermute | solution.py:25
  354.9 10.1 %collective-permute-start.8 = (bf16[128,1,10,66]{3,2,1,0:T(8,128)(2,1)}, bf16[128,1,10,66]{3,2,1,0:T(8,128)(2,1)S(1)}, u32[]{:S(2)}, u32[]{:S(2)}) collective-permute-start(bf16[128,1,10,66]{3,2,1,0:T(8,128)(2,1)} %get-tuple-element.8), channel_id=1, source_target_pairs={{1,0},{2,1},{3,2},{5,4},{6,5},{7,6},{9,8},{10,9},{11,10},{13,12},{... | collective-permute-start | bytes 506888 | tf_op jit(solution)/shard_map/ppermute | solution.py:26
where the time goes:
time: 378 us; the launch traced here: 372 us
  blocking collectives  197 us (52%)
  local copies, waits for them, and re-layouts  72.9 us (19%)
  waiting for transfers between devices  35.6 us (9%)
  starting transfers between devices  32.6 us (9%)
  other arithmetic  20.5 us (5%)
  matrix products  12.3 us (3%)
    psum x1, blocking collectives, body(): channel_total = lax.psum(jnp.sum(grouped, axis=2), ('gx', 'gy', 'gz'))  103 us
    psum x1, blocking collectives, body(): covariance = lax.psum(moments, ('gx', 'gy', 'gz')) / total_cells  94.6 us
    unnamed x20, local copies, waits for them, and re-layouts  21.1 us
    conv_general_dilated x8, local copies, waits for them, and re-layouts, convolve(): lax.conv_general_dilated(volume[None], kernel, strides, ((0, 0), (0, 0),...  18.6 us
    ppermute x3, waiting for transfers between devices, from_behind(): lax.ppermute(value, axis, [(source, source + steps) for source in range(l...  15.2 us
    ppermute x3, waiting for transfers between devices, extended_2(): after = lax.ppermute(leading, axis, down)  14.9 us
    ppermute x3, starting transfers between devices, from_behind(): lax.ppermute(value, axis, [(source, source + steps) for source in range(l...  13.9 us
    ppermute x3, starting transfers between devices, extended_2(): before = lax.ppermute(last, axis, up)  13.2 us
  transfers between devices with their start and end apart: 9, of which 7 were waited for; matrix products, arithmetic and copies ran while one was open for 2% of the time, Pallas kernels for 0%

commit v1 on v0

--- a/solution.py
+++ b/solution.py
@@ -82,7 +82,7 @@
     average = channel_total / total_cells
     centered = grouped - average[:, :, None]
     moments = jnp.einsum("gim,gjm->gij", centered, centered, precision=lax.Precision.HIGHEST)
-    covariance = lax.psum(moments, ("gx", "gy", "gz")) / total_cells
+    covariance = lax.psum(lax.psum(moments, "gx"), ("gy", "gz")) / total_cells
     covariance = covariance + epsilon * identity
     whitener = newton_whitener(covariance)
     activation = whiten(features, average, whitener, norm_gain, norm_shift)

time: 378 us -> 556 us (1.47)
  the two profiles are of different devices: /device:TPU:15 before, /device:TPU:7 now
where the time goes in v1:
time: 556 us; the launch traced here: 551 us
  blocking collectives  373 us (67%)
  local copies, waits for them, and re-layouts  73 us (13%)
  starting transfers between devices  39.8 us (7%)
  waiting for transfers between devices  31.4 us (6%)
  other arithmetic  20.5 us (4%)
  matrix products  12.3 us (2%)
    psum x2, blocking collectives, body(): covariance = lax.psum(lax.psum(moments, 'gx'), ('gy', 'gz')) / total_cells  268 us
    psum x1, blocking collectives, body(): channel_total = lax.psum(jnp.sum(grouped, axis=2), ('gx', 'gy', 'gz'))  105 us
    unnamed x20, local copies, waits for them, and re-layouts  21.1 us
    conv_general_dilated x8, local copies, waits for them, and re-layouts, convolve(): lax.conv_general_dilated(volume[None], kernel, strides, ((0, 0), (0, 0),...  18.6 us
    ppermute x3, starting transfers between devices, from_behind(): lax.ppermute(value, axis, [(source, source + steps) for source in range(l...  17.6 us
    ppermute x3, waiting for transfers between devices, extended_2(): after = lax.ppermute(leading, axis, down)  17.4 us
    ppermute x3, starting transfers between devices, extended_2(): before = lax.ppermute(last, axis, up)  17.3 us
  transfers between devices with their start and end apart: 9, of which 7 were waited for; matrix products, arithmetic and copies ran while one was open for 2% of the time, Pallas kernels for 0%

profile of v1, /device:TPU:7, one launch (start us, length us, event | category | flops | bytes accessed | tf_op | source)
XLA Modules:
  0.0 550.6 jit_solution(15632235082247535100)
XLA Ops:
  4.7 4.0 collective-permute-start
  11.0 4.3 copy.42
  16.6 8.2 %collective-permute-start.1 = (bf16[64,8,1,129]{3,1,2,0:T(8,128)(2,1)S(1)}, bf16[64,8,1,129]{3,1,2,0:T(8,128)(2,1)S(1)}, u32[]{:S(2)}, u32[]{:S(2)}) collective-permute-start(bf16[64,8,1,129]{3,1,2,0:T(8,128)(2,1)S(1)} %pad_maximum_fusion.6), channel_id=1, source_target_pairs={{0,4},{4,8},{8,12},{12,16},{16,20},{20,24},{24,28},{28,32},{32,36}... | collective-permute-start | bytes 396296 | tf_op jit(solution)/shard_map/ppermute | solution.py:15
  24.8 3.3 collective-permute-done.1
  28.1 2.5 pad_maximum_fusion.1
  30.7 5.4 collective-permute-start.2
  36.4 7.6 %collective-permute-done.2 = bf16[64,1,17,129]{3,0,2,1:T(8,128)(2,1)S(1)} collective-permute-done((bf16[64,1,17,129]{3,0,2,1:T(8,128)(2,1)S(1)}, bf16[64,1,17,129]{3,0,2,1:T(8,128)(2,1)S(1)}, u32[]{:S(2)}, u32[]{:S(2)}) %collective-permute-start.2) | collective-permute-done | bytes 280736 | tf_op jit(solution)/shard_map/ppermute | solution.py:15
  44.8 7.4 %maximum_bitcast_fusion = bf16[64,9,17,1,129]{4,1,2,0,3:T(8,128)(2,1)} fusion(bf16[64,8,16,128]{3,1,2,0:T(8,128)(2,1)S(1)} %copy.43, bf16[64,8,16,1]{3,1,2,0:T(8,128)(2,1)S(1)} %copy-done.1, bf16[64,8,1,129]{3,1,2,0:T(8,128)(2,1)S(1)} %collective-permute-done.1, bf16[64,1,17,129]{3,1,2,0:T(2,128)(2,1)S(1)} %copy.45), kind=kLoop, calls=%fused_computation.2 | loop fusion | flops 10105344 | bytes 5052672 | tf_op jit(solution)/shard_map/broadcast_in_dim | solution.py:33
  52.3 14.9 %copy.64 = bf16[64,9,17,1,129]{0,4,2,1,3:T(8,128)(2,1)} copy(bf16[64,9,17,1,129]{4,1,2,0,3:T(8,128)(2,1)} %maximum_bitcast_fusion) | data formatting | bytes 5052672
  67.2 6.0 %pad.clone = bf16[64,9,17,1,144]{0,4,2,1,3:T(8,128)(2,1)} pad(bf16[64,9,17,1,129]{0,4,2,1,3:T(8,128)(2,1)} %copy.64, bf16[]{:T(256)} %constant.22), padding=0_0x0_0x0_0x0_0x0_15 | pad | bytes 5346434 | tf_op jit(solution)/shard_map/broadcast_in_dim | solution.py:33
  73.2 10.6 %reshape.24 = bf16[64,9,17,1,8,18]{0,5,4,2,1,3:T(8,128)(2,1)} reshape(bf16[64,9,17,1,144]{0,4,2,1,3:T(8,128)(2,1)} %pad.clone) | data formatting | bytes 5640192 | tf_op jit(solution)/shard_map/conv_general_dilated | solution.py:32
  83.9 4.3 copy.48
  88.4 2.9 select_reduce_fusion
  91.6 3.0 copy.50
  96.7 104.9 %psum.21 = f32[2,64]{1,0:T(2,128)S(1)} all-reduce(f32[2,64]{1,0:T(2,128)S(1)} %reduce_sum.22), channel_id=1, replica_groups=mesh['gx'=8,'gy'=16,'gz'=4] {'gx','gy','gz'}, use_global_device_ids=true, to_apply=%region_1.0 | all-reduce | flops 128 | bytes 1024 | tf_op jit(solution)/shard_map/psum | solution.py:81
  202.8 21.7 %psum.22 = f32[2,64,64]{2,1,0:T(8,128)S(1)} all-reduce(f32[2,64,64]{2,1,0:T(8,128)S(1)} %fusion.32), channel_id=1, replica_groups=mesh['gx'=8,'gy'=16,'gz'=4] {'gx'}, use_global_device_ids=true, to_apply=%region_2.0 | all-reduce | flops 8192 | bytes 65536 | tf_op jit(solution)/shard_map/psum | solution.py:85
  224.6 246.3 %psum.23 = f32[2,64,64]{2,1,0:T(8,128)S(1)} all-reduce(f32[2,64,64]{2,1,0:T(8,128)S(1)} %psum.22), channel_id=1, replica_groups=mesh['gx'=8,'gy'=16,'gz'=4] {'gy','gz'}, use_global_device_ids=true, to_apply=%region_3.0 | all-reduce | flops 8192 | bytes 65536 | tf_op jit(solution)/shard_map/psum | solution.py:85
  492.0 3.7 pad_maximum_fusion.5
  495.7 14.7 %collective-permute-start.5 = (bf16[128,4,1,66]{3,2,1,0:T(2,128)(2,1)S(1)}, bf16[128,4,1,66]{3,2,1,0:T(2,128)(2,1)S(1)}, u32[]{:S(2)}, u32[]{:S(2)}) collective-permute-start(bf16[128,4,1,66]{3,2,1,0:T(2,128)(2,1)S(1)} %get-tuple-element.5), channel_id=1, source_target_pairs={{0,4},{4,8},{8,12},{12,16},{16,20},{20,24},{24,28},{28,32},{32,36}... | collective-permute-start | bytes 202760 | tf_op jit(solution)/shard_map/ppermute | solution.py:25
  513.7 12.7 %collective-permute-done.6 = bf16[128,4,1,66]{3,2,1,0:T(2,128)(2,1)S(1)} collective-permute-done((bf16[128,4,1,66]{3,2,1,0:T(2,128)(2,1)S(1)}, bf16[128,4,1,66]{3,2,1,0:T(2,128)(2,1)S(1)}, u32[]{:S(2)}, u32[]{:S(2)}) %collective-permute-start.6) | collective-permute-done | bytes 67616 | tf_op jit(solution)/shard_map/ppermute | solution.py:26
  526.4 3.3 pad_maximum_fusion
  535.0 3.1 copy.56
  540.3 3.4 collective-permute-done.8
  545.1 4.3 fusion.18
  (80 shorter events, 47.4 us)
Async XLA Ops:
  0.0 545.1 %copy-start = (bf16[3,3,3,128,128]{4,3,2,1,0:T(8,128)(2,1)S(1)}, bf16[3,3,3,128,128]{4,3,2,1,0:T(8,128)(2,1)}, u32[]{:S(2)}) copy-start(bf16[3,3,3,128,128]{4,3,2,1,0:T(8,128)(2,1)} %param.9) | copy-start | bytes 2654212
  4.7 6.4 %collective-permute-start = (bf16[64,8,16,1]{0,2,3,1:T(8,128)(2,1)S(1)}, bf16[64,8,16,1]{0,2,3,1:T(8,128)(2,1)S(1)}, u32[]{:S(2)}, u32[]{:S(2)}) collective-permute-start(bf16[64,8,16,1]{0,2,3,1:T(8,128)(2,1)S(1)} %copy.63), channel_id=1, source_target_pairs={{0,64},{64,128},{128,192},{192,256},{256,320},{320,384},{384,448},... | collective-permute-start | bytes 49160 | tf_op jit(solution)/shard_map/ppermute | solution.py:15
  15.4 12.7 %copy-start.1 = (bf16[64,8,16,1]{3,1,2,0:T(8,128)(2,1)S(1)}, bf16[64,8,16,1]{3,1,2,0:T(8,128)(2,1)}, u32[]{:S(2)}) copy-start(bf16[64,8,16,1]{3,1,2,0:T(8,128)(2,1)} %copy.42) | copy-start | bytes 49156
  16.6 11.5 %collective-permute-start.1 = (bf16[64,8,1,129]{3,1,2,0:T(8,128)(2,1)S(1)}, bf16[64,8,1,129]{3,1,2,0:T(8,128)(2,1)S(1)}, u32[]{:S(2)}, u32[]{:S(2)}) collective-permute-start(bf16[64,8,1,129]{3,1,2,0:T(8,128)(2,1)S(1)} %pad_maximum_fusion.6), channel_id=1, source_target_pairs={{0,4},{4,8},{8,12},{12,16},{16,20},{20,24},{24,28},{28,32},{32,36}... | collective-permute-start | bytes 396296 | tf_op jit(solution)/shard_map/ppermute | solution.py:15
  30.7 13.2 %collective-permute-start.2 = (bf16[64,1,17,129]{3,0,2,1:T(8,128)(2,1)S(1)}, bf16[64,1,17,129]{3,0,2,1:T(8,128)(2,1)S(1)}, u32[]{:S(2)}, u32[]{:S(2)}) collective-permute-start(bf16[64,1,17,129]{3,0,2,1:T(8,128)(2,1)S(1)} %copy.44), channel_id=1, source_target_pairs={{0,1},{1,2},{2,3},{4,5},{5,6},{6,7},{8,9},{9,10},{10,11},{12,13},{... | collective-permute-start | bytes 842120 | tf_op jit(solution)/shard_map/ppermute | solution.py:15
  83.8 4.5 copy-start.6
  83.8 4.5 copy-start.7
  474.7 2.2 copy-start.4
  474.7 2.2 copy-start.5
  482.8 3.9 collective-permute-start.3
  485.2 4.4 collective-permute-start.4
  492.0 34.4 %copy-start.3 = (bf16[128,4,8,1]{3,2,1,0:T(8,128)(2,1)S(1)}, bf16[128,4,8,1]{3,2,1,0:T(8,128)(2,1)}, u32[]{:S(2)}) copy-start(bf16[128,4,8,1]{3,2,1,0:T(8,128)(2,1)} %copy.54) | copy-start | bytes 24580
  495.7 18.0 %collective-permute-start.5 = (bf16[128,4,1,66]{3,2,1,0:T(2,128)(2,1)S(1)}, bf16[128,4,1,66]{3,2,1,0:T(2,128)(2,1)S(1)}, u32[]{:S(2)}, u32[]{:S(2)}) collective-permute-start(bf16[128,4,1,66]{3,2,1,0:T(2,128)(2,1)S(1)} %get-tuple-element.5), channel_id=1, source_target_pairs={{0,4},{4,8},{8,12},{12,16},{16,20},{20,24},{24,28},{28,32},{32,36}... | collective-permute-start | bytes 202760 | tf_op jit(solution)/shard_map/ppermute | solution.py:25
  510.4 16.0 %collective-permute-start.6 = (bf16[128,4,1,66]{3,2,1,0:T(2,128)(2,1)S(1)}, bf16[128,4,1,66]{3,2,1,0:T(2,128)(2,1)S(1)}, u32[]{:S(2)}, u32[]{:S(2)}) collective-permute-start(bf16[128,4,1,66]{3,2,1,0:T(2,128)(2,1)S(1)} %get-tuple-element.6), channel_id=1, source_target_pairs={{4,0},{8,4},{12,8},{16,12},{20,16},{24,20},{28,24},{32,28},{36,32}... | collective-permute-start | bytes 202760 | tf_op jit(solution)/shard_map/ppermute | solution.py:26
  529.7 1.4 copy-start.2
  532.2 7.7 %collective-permute-start.7 = (bf16[128,1,10,66]{3,2,1,0:T(8,128)(2,1)}, bf16[128,1,10,66]{3,2,1,0:T(8,128)(2,1)S(1)}, u32[]{:S(2)}, u32[]{:S(2)}) collective-permute-start(bf16[128,1,10,66]{3,2,1,0:T(8,128)(2,1)} %get-tuple-element.7), channel_id=1, source_target_pairs={{0,1},{1,2},{2,3},{4,5},{5,6},{6,7},{8,9},{9,10},{10,11},{12,13},{... | collective-permute-start | bytes 506888 | tf_op jit(solution)/shard_map/ppermute | solution.py:25
  533.5 10.1 %collective-permute-start.8 = (bf16[128,1,10,66]{3,2,1,0:T(8,128)(2,1)}, bf16[128,1,10,66]{3,2,1,0:T(8,128)(2,1)S(1)}, u32[]{:S(2)}, u32[]{:S(2)}) collective-permute-start(bf16[128,1,10,66]{3,2,1,0:T(8,128)(2,1)} %get-tuple-element.8), channel_id=1, source_target_pairs={{1,0},{2,1},{3,2},{5,4},{6,5},{7,6},{9,8},{10,9},{11,10},{13,12},{... | collective-permute-start | bytes 506888 | tf_op jit(solution)/shard_map/ppermute | solution.py:26
